TPU v7x, 128 devices: a whole 4x4x4 slice. The times are simulated.
128 devices in a mesh: section: 4 (over z), mp: 32 (over y, x, core).
Axes of the slice: x: 4, y: 4, z: 4, core: 2. Of those that a mesh axis runs over, the one named last changes fastest.
Arguments:
- entering_hidden: bfloat16 [4, 256, 8192], P('section', None, 'mp'), may hold values from -12 to 12
- section_weight: bfloat16 [4, 8192, 8192], P('section', None, 'mp'), may hold values from -0.0625 to 0.0625
- section_norm_gain: bfloat16 [4, 8192], P('section', 'mp'), may hold values from 0.5 to 1.5
- plugin_narrowing_factors: bfloat16 [4, 32, 8192, 64], P('section', 'mp'), may hold values from -0.0625 to 0.0625
- plugin_widening_factors: bfloat16 [4, 32, 64, 8192], P('section', 'mp'), may hold values from -0.75 to 0.75
- reward_head: bfloat16 [8192], P('mp'), may hold values from -0.0625 to 0.0625
- adapter_of_block: int32 [4, 2], replicated, may hold values from 0 to 31
- live_block_rows: int32 [4, 2], P('section'), may hold values from 1 to 128
Outputs:
- hidden_out: bfloat16 [4, 256, 8192], P('section', None, 'mp')
- scores: float32 [4, 256], P('section')
All inputs are finite; a program needn't handle non-finite values.
Results may differ from a plain program's by a relative error of at most 0.022.
Values may be sent and summed in bfloat16 or wider, within the bound.
A program may use at most 64 MiB of HBM per device.

v0:
```python
import jax
import jax.numpy as jnp
from jax import lax
from jax.sharding import PartitionSpec as P

BLOCK = 128


def shifted(value, axis, steps):
    count = lax.axis_size(axis)
    initial, last = (max(0, -steps), min(count, count - steps))
    return lax.ppermute(value, axis, [(source, source + steps) for source in range(initial, last)])


def shards(
    entering_hidden,
    section_weight,
    section_norm_gain,
    plugin_narrowing_factors,
    plugin_widening_factors,
    reward_head,
    adapter_of_block,
    live_block_rows,
):
    sections = lax.axis_size("section")
    section_index = lax.axis_index("section")
    owners = lax.axis_size("mp")
    owner_index = lax.axis_index("mp")
    batches_here, rows, piece_extent = entering_hidden.shape
    micro = batches_here * sections
    width = piece_extent * owners
    blocks = rows // BLOCK
    owned_blocks = plugin_narrowing_factors.shape[1]
    adapters = owned_blocks * owners
    rank_position = plugin_narrowing_factors.shape[3]
    weight = section_weight[0]
    gain = section_norm_gain[0].astype(jnp.float32)
    fed = lax.all_gather(entering_hidden, "section", axis=0, tiled=True)
    up_map_columns = lax.all_to_all(
        plugin_widening_factors, "mp", split_axis=3, concat_axis=1, tiled=True
    )[0]
    up_table = up_map_columns.reshape(adapters, rank_position * piece_extent)

    def layer_of_section(hidden_state, adapter_numbers):
        hidden_f = hidden_state.astype(jnp.float32)
        onehot = (
            adapter_numbers[:, None] == jnp.arange(adapters, dtype=jnp.int32)[None, :]
        ).astype(jnp.bfloat16)
        squares = lax.psum(jnp.sum(hidden_f * hidden_f, axis=1), "mp")
        rescaled_activation = (
            hidden_f * lax.rsqrt(squares / width + 1e-05)[:, None] * gain[None, :]
        ).astype(jnp.bfloat16)
        gathered = lax.all_gather(rescaled_activation, "mp", axis=1, tiled=True)
        base = jnp.dot(gathered, weight, preferred_element_type=jnp.float32)
        local_ids = adapter_numbers - owner_index * owned_blocks
        mine = (local_ids >= 0) & (local_ids < owned_blocks)
        products = []
        for block_number in range(blocks):
            segment = gathered[block_number * BLOCK : (block_number + 1) * BLOCK]
            picked = jnp.clip(local_ids[block_number], 0, owned_blocks - 1)
            products.append(
                lax.cond(
                    mine[block_number],
                    lambda incoming_rows, selected_adapter: jnp.dot(
                        incoming_rows,
                        plugin_narrowing_factors[0, selected_adapter],
                        preferred_element_type=jnp.float32,
                    ),
                    lambda incoming_rows, selected_adapter: jnp.zeros(
                        (BLOCK, rank_position), jnp.float32
                    ),
                    segment,
                    picked,
                )
            )
        compressed_projection = jnp.stack(products)
        compressed_projection = lax.psum(compressed_projection.astype(jnp.bfloat16), "mp")
        chosen_expansion_matrix = (
            jnp.dot(onehot, up_table, preferred_element_type=jnp.float32)
            .astype(jnp.bfloat16)
            .reshape(blocks, rank_position, piece_extent)
        )
        thin_correction = jnp.einsum(
            "sin,sny->siy",
            compressed_projection,
            chosen_expansion_matrix,
            preferred_element_type=jnp.float32,
        ).reshape(rows, piece_extent)
        return (hidden_f + base + 2.0 * thin_correction).astype(jnp.bfloat16)

    def tick(step, carry):
        moving, finished = carry
        arrived = shifted(moving, "section", 1)
        feed_now = lax.dynamic_index_in_dim(fed, jnp.minimum(step, micro - 1), 0, keepdims=False)
        current_signal = jnp.where(section_index == 0, feed_now, arrived)
        selected_adapter = step - section_index
        valid = (selected_adapter >= 0) & (selected_adapter < micro)
        position = jnp.clip(selected_adapter, 0, micro - 1)
        adapter_numbers = lax.dynamic_index_in_dim(adapter_of_block, position, 0, keepdims=False)
        output = layer_of_section(current_signal, adapter_numbers)
        entry_tuple = valid & (section_index == sections - 1)
        previous = lax.dynamic_index_in_dim(finished, position, 0, keepdims=False)
        finished = lax.dynamic_update_index_in_dim(
            finished, jnp.where(entry_tuple, output, previous), position, 0
        )
        return (output, finished)

    start_moving = jnp.zeros((rows, piece_extent), jnp.bfloat16)
    start_finished = jnp.zeros((micro, rows, piece_extent), jnp.bfloat16)
    moving, finished = lax.fori_loop(0, micro + sections - 1, tick, (start_moving, start_finished))
    hidden_out = lax.psum_scatter(
        finished.astype(jnp.float32).astype(jnp.bfloat16),
        "section",
        scatter_dimension=0,
        tiled=True,
    )
    partial_score = jnp.sum(
        hidden_out.astype(jnp.float32) * reward_head.astype(jnp.float32)[None, None, :], axis=2
    )
    raw = lax.psum(partial_score, "mp")
    place = jnp.arange(rows, dtype=jnp.int32) % BLOCK
    limits = jnp.repeat(live_block_rows, BLOCK, axis=1)
    scores = jnp.where(place[None, :] < limits, raw, jnp.float32(0.0))
    return (hidden_out, scores)


def solution(mesh):
    placed = (
        P("section", None, "mp"),
        P("section", None, "mp"),
        P("section", "mp"),
        P("section", "mp", None, None),
        P("section", "mp", None, None),
        P("mp"),
        P(),
        P("section", None),
    )
    return jax.shard_map(
        shards,
        mesh=mesh,
        in_specs=placed,
        out_specs=(P("section", None, "mp"), P("section", None)),
        check_vma=False,
    )
```

profile of v0, /device:TPU:0, one launch (start us, length us, event | category | flops | bytes accessed | tf_op | source)
XLA Modules:
  0.0 1954.4 jit_solution(13879705828689722286)
XLA Ops:
  17.7 45.2 %reduce.1 = bf16[8192,64]{1,0:T(8,128)(2,1)S(1)} reduce(bf16[8192,1,1,64]{3,2,1,0:T(2,128)(2,1)} %bitcast.80, bf16[]{:T(256)} %broadcast.105), dimensions={1,2}, to_apply=%bitcast.49.reduce_sub_computation | reduce | bytes 2097154
  106.2 1752.9 %while.17 = (s32[]{:T(128)}, bf16[256,256]{1,0:T(8,128)(2,1)}, bf16[4,256,256]{2,1,0:T(8,128)(2,1)}, pred[]{:T(512)}, bf16[4,256,256]{2,1,0:T(8,128)(2,1)}, /*in...) while((s32[]{:T(128)}, bf16[256,256]{1,0:T(8,128)(2,1)}, ...), condition=%wide.region_8.9_spmd.clone, body=%wide.region_0.8_spmd.clone.sunk | while | flops 1353712128 | bytes 31792572 | solution.py:110
  114.1 63.3 %psum.36 = f32[256]{0:T(256)S(1)} all-reduce(f32[256]{0:T(256)S(1)} %get-tuple-element.499), channel_id=1, replica_groups=mesh['section'=4,'mp'=32] {'mp'}, use_global_device_ids=true, to_apply=%region_2.2 | all-reduce | flops 256 | bytes 2048 | tf_op jit(solution)/shard_map/while/body/eval_jaxpr/psum | solution.py:49
  181.2 43.1 %all-gather.2.cloned.1.call-done = bf16[256,8192]{1,0:T(8,128)(2,1)} async-done(((bf16[256,256]{1,0:T(8,128)(2,1)}), bf16[256,8192]{1,0:T(8,128)(2,1)}) %all-gather.2.cloned.1.call-update) | async-done | bytes 4194320 | tf_op jit(solution)/shard_map/while/body/eval_jaxpr/all_gather | solution.py:53
  224.3 126.5 %psum.37 = bf16[2,128,64]{1,2,0:T(8,128)(2,1)S(1)} all-reduce(bf16[2,128,64]{1,2,0:T(8,128)(2,1)S(1)} %pad_maximum_fusion.2), channel_id=1, replica_groups=mesh['section'=4,'mp'=32] {'mp'}, use_global_device_ids=true, to_apply=%region_7.7 | all-reduce | flops 16384 | bytes 65536 | tf_op jit(solution)/shard_map/while/body/eval_jaxpr/psum | solution.py:77
  364.4 62.7 %psum.36 = f32[256]{0:T(256)S(1)} all-reduce(f32[256]{0:T(256)S(1)} %get-tuple-element.499), channel_id=1, replica_groups=mesh['section'=4,'mp'=32] {'mp'}, use_global_device_ids=true, to_apply=%region_2.2 | all-reduce | flops 256 | bytes 2048 | tf_op jit(solution)/shard_map/while/body/eval_jaxpr/psum | solution.py:49
  430.9 42.9 %all-gather.2.cloned.1.call-done = bf16[256,8192]{1,0:T(8,128)(2,1)} async-done(((bf16[256,256]{1,0:T(8,128)(2,1)}), bf16[256,8192]{1,0:T(8,128)(2,1)}) %all-gather.2.cloned.1.call-update) | async-done | bytes 4194320 | tf_op jit(solution)/shard_map/while/body/eval_jaxpr/all_gather | solution.py:53
  476.4 123.8 %psum.37 = bf16[2,128,64]{1,2,0:T(8,128)(2,1)S(1)} all-reduce(bf16[2,128,64]{1,2,0:T(8,128)(2,1)S(1)} %pad_maximum_fusion.2), channel_id=1, replica_groups=mesh['section'=4,'mp'=32] {'mp'}, use_global_device_ids=true, to_apply=%region_7.7 | all-reduce | flops 16384 | bytes 65536 | tf_op jit(solution)/shard_map/while/body/eval_jaxpr/psum | solution.py:77
  613.8 62.7 %psum.36 = f32[256]{0:T(256)S(1)} all-reduce(f32[256]{0:T(256)S(1)} %get-tuple-element.499), channel_id=1, replica_groups=mesh['section'=4,'mp'=32] {'mp'}, use_global_device_ids=true, to_apply=%region_2.2 | all-reduce | flops 256 | bytes 2048 | tf_op jit(solution)/shard_map/while/body/eval_jaxpr/psum | solution.py:49
  680.3 42.9 %all-gather.2.cloned.1.call-done = bf16[256,8192]{1,0:T(8,128)(2,1)} async-done(((bf16[256,256]{1,0:T(8,128)(2,1)}), bf16[256,8192]{1,0:T(8,128)(2,1)}) %all-gather.2.cloned.1.call-update) | async-done | bytes 4194320 | tf_op jit(solution)/shard_map/while/body/eval_jaxpr/all_gather | solution.py:53
  723.2 129.1 %psum.37 = bf16[2,128,64]{1,2,0:T(8,128)(2,1)S(1)} all-reduce(bf16[2,128,64]{1,2,0:T(8,128)(2,1)S(1)} %pad_maximum_fusion.2), channel_id=1, replica_groups=mesh['section'=4,'mp'=32] {'mp'}, use_global_device_ids=true, to_apply=%region_7.7 | all-reduce | flops 16384 | bytes 65536 | tf_op jit(solution)/shard_map/while/body/eval_jaxpr/psum | solution.py:77
  863.7 62.7 %psum.36 = f32[256]{0:T(256)S(1)} all-reduce(f32[256]{0:T(256)S(1)} %get-tuple-element.499), channel_id=1, replica_groups=mesh['section'=4,'mp'=32] {'mp'}, use_global_device_ids=true, to_apply=%region_2.2 | all-reduce | flops 256 | bytes 2048 | tf_op jit(solution)/shard_map/while/body/eval_jaxpr/psum | solution.py:49
  930.2 42.4 %all-gather.2.cloned.1.call-done = bf16[256,8192]{1,0:T(8,128)(2,1)} async-done(((bf16[256,256]{1,0:T(8,128)(2,1)}), bf16[256,8192]{1,0:T(8,128)(2,1)}) %all-gather.2.cloned.1.call-update) | async-done | bytes 4194320 | tf_op jit(solution)/shard_map/while/body/eval_jaxpr/all_gather | solution.py:53
  972.6 126.5 %psum.37 = bf16[2,128,64]{1,2,0:T(8,128)(2,1)S(1)} all-reduce(bf16[2,128,64]{1,2,0:T(8,128)(2,1)S(1)} %pad_maximum_fusion.2), channel_id=1, replica_groups=mesh['section'=4,'mp'=32] {'mp'}, use_global_device_ids=true, to_apply=%region_7.7 | all-reduce | flops 16384 | bytes 65536 | tf_op jit(solution)/shard_map/while/body/eval_jaxpr/psum | solution.py:77
  1115.3 62.7 %psum.36 = f32[256]{0:T(256)S(1)} all-reduce(f32[256]{0:T(256)S(1)} %get-tuple-element.499), channel_id=1, replica_groups=mesh['section'=4,'mp'=32] {'mp'}, use_global_device_ids=true, to_apply=%region_2.2 | all-reduce | flops 256 | bytes 2048 | tf_op jit(solution)/shard_map/while/body/eval_jaxpr/psum | solution.py:49
  1181.8 41.3 %all-gather.2.cloned.1.call-done = bf16[256,8192]{1,0:T(8,128)(2,1)} async-done(((bf16[256,256]{1,0:T(8,128)(2,1)}), bf16[256,8192]{1,0:T(8,128)(2,1)}) %all-gather.2.cloned.1.call-update) | async-done | bytes 4194320 | tf_op jit(solution)/shard_map/while/body/eval_jaxpr/all_gather | solution.py:53
  1223.1 126.5 %psum.37 = bf16[2,128,64]{1,2,0:T(8,128)(2,1)S(1)} all-reduce(bf16[2,128,64]{1,2,0:T(8,128)(2,1)S(1)} %pad_maximum_fusion.2), channel_id=1, replica_groups=mesh['section'=4,'mp'=32] {'mp'}, use_global_device_ids=true, to_apply=%region_7.7 | all-reduce | flops 16384 | bytes 65536 | tf_op jit(solution)/shard_map/while/body/eval_jaxpr/psum | solution.py:77
  1363.1 62.7 %psum.36 = f32[256]{0:T(256)S(1)} all-reduce(f32[256]{0:T(256)S(1)} %get-tuple-element.499), channel_id=1, replica_groups=mesh['section'=4,'mp'=32] {'mp'}, use_global_device_ids=true, to_apply=%region_2.2 | all-reduce | flops 256 | bytes 2048 | tf_op jit(solution)/shard_map/while/body/eval_jaxpr/psum | solution.py:49
  1429.6 45.5 %all-gather.2.cloned.1.call-done = bf16[256,8192]{1,0:T(8,128)(2,1)} async-done(((bf16[256,256]{1,0:T(8,128)(2,1)}), bf16[256,8192]{1,0:T(8,128)(2,1)}) %all-gather.2.cloned.1.call-update) | async-done | bytes 4194320 | tf_op jit(solution)/shard_map/while/body/eval_jaxpr/all_gather | solution.py:53
  1475.2 126.5 %psum.37 = bf16[2,128,64]{1,2,0:T(8,128)(2,1)S(1)} all-reduce(bf16[2,128,64]{1,2,0:T(8,128)(2,1)S(1)} %pad_maximum_fusion.2), channel_id=1, replica_groups=mesh['section'=4,'mp'=32] {'mp'}, use_global_device_ids=true, to_apply=%region_7.7 | all-reduce | flops 16384 | bytes 65536 | tf_op jit(solution)/shard_map/while/body/eval_jaxpr/psum | solution.py:77
  1615.2 62.7 %psum.36 = f32[256]{0:T(256)S(1)} all-reduce(f32[256]{0:T(256)S(1)} %get-tuple-element.499), channel_id=1, replica_groups=mesh['section'=4,'mp'=32] {'mp'}, use_global_device_ids=true, to_apply=%region_2.2 | all-reduce | flops 256 | bytes 2048 | tf_op jit(solution)/shard_map/while/body/eval_jaxpr/psum | solution.py:49
  1681.7 45.3 %all-gather.2.cloned.1.call-done = bf16[256,8192]{1,0:T(8,128)(2,1)} async-done(((bf16[256,256]{1,0:T(8,128)(2,1)}), bf16[256,8192]{1,0:T(8,128)(2,1)}) %all-gather.2.cloned.1.call-update) | async-done | bytes 4194320 | tf_op jit(solution)/shard_map/while/body/eval_jaxpr/all_gather | solution.py:53
  1727.0 126.5 %psum.37 = bf16[2,128,64]{1,2,0:T(8,128)(2,1)S(1)} all-reduce(bf16[2,128,64]{1,2,0:T(8,128)(2,1)S(1)} %pad_maximum_fusion.2), channel_id=1, replica_groups=mesh['section'=4,'mp'=32] {'mp'}, use_global_device_ids=true, to_apply=%region_7.7 | all-reduce | flops 16384 | bytes 65536 | tf_op jit(solution)/shard_map/while/body/eval_jaxpr/psum | solution.py:77
  1881.8 64.6 %psum.31 = f32[1,256]{1,0:T(1,128)S(1)} all-reduce(f32[1,256]{1,0:T(1,128)S(1)} %bitcast.87), channel_id=1, replica_groups=mesh['section'=4,'mp'=32] {'mp'}, use_global_device_ids=true, to_apply=%region_11.12 | all-reduce | flops 256 | bytes 2048 | tf_op jit(solution)/shard_map/psum | solution.py:120
  (165 shorter events, 195.2 us)
Async XLA Ops:
  62.9 11.8 copy-start.1
  62.9 11.9 copy-start.2
  62.9 11.9 copy-start
  65.2 24.6 %all-to-all-start = ((bf16[32,2,8192]{2,1,0:T(2,128)(2,1)}), bf16[32,2,8192]{2,1,0:T(2,128)(2,1)S(1)}, u32[]{:S(2)}, u32[]{:S(2)}) async-start(bf16[32,2,8192]{2,1,0:T(2,128)(2,1)} %reshape.80), calls=%async_computation | async-start | bytes 2097152 | tf_op jit(solution)/shard_map/all_to_all | solution.py:39
  106.2 1753.5 %copy-start.3 = (bf16[256]{0:T(256)(128)(2,1)S(1)}, bf16[256]{0:T(256)(128)(2,1)}, u32[]{:S(2)}) copy-start(bf16[256]{0:T(256)(128)(2,1)} %param.19) | copy-start | bytes 1540
  106.2 1840.2 %copy-start.4 = (s32[1,2]{1,0:T(1,128)S(1)}, s32[1,2]{1,0:T(1,128)}, u32[]{:S(2)}) copy-start(s32[1,2]{1,0:T(1,128)} %param.21) | copy-start | bytes 28
  106.2 118.1 %all-gather.2.cloned.1.call-start = ((), (), s32[]{:S(2)}) async-start(), calls=%async_computation.3 | async-start | bytes 4325376 | tf_op jit(solution)/shard_map/while/body/eval_jaxpr/all_gather | solution.py:53
  106.2 6.8 collective-permute-start
  356.4 117.3 %all-gather.2.cloned.1.call-start = ((), (), s32[]{:S(2)}) async-start(), calls=%async_computation.3 | async-start | bytes 4325376 | tf_op jit(solution)/shard_map/while/body/eval_jaxpr/all_gather | solution.py:53
  357.4 6.0 collective-permute-start
  605.9 117.3 %all-gather.2.cloned.1.call-start = ((), (), s32[]{:S(2)}) async-start(), calls=%async_computation.3 | async-start | bytes 4325376 | tf_op jit(solution)/shard_map/while/body/eval_jaxpr/all_gather | solution.py:53
  606.8 6.0 collective-permute-start
  857.9 114.7 %all-gather.2.cloned.1.call-start = ((), (), s32[]{:S(2)}) async-start(), calls=%async_computation.3 | async-start | bytes 4325376 | tf_op jit(solution)/shard_map/while/body/eval_jaxpr/all_gather | solution.py:53
  858.8 3.8 collective-permute-start
  1104.7 118.4 %all-gather.2.cloned.1.call-start = ((), (), s32[]{:S(2)}) async-start(), calls=%async_computation.3 | async-start | bytes 4325376 | tf_op jit(solution)/shard_map/while/body/eval_jaxpr/all_gather | solution.py:53
  1105.7 8.6 collective-permute-start
  1355.2 119.9 %all-gather.2.cloned.1.call-start = ((), (), s32[]{:S(2)}) async-start(), calls=%async_computation.3 | async-start | bytes 4325376 | tf_op jit(solution)/shard_map/while/body/eval_jaxpr/all_gather | solution.py:53
  1356.1 6.0 collective-permute-start
  1607.3 119.7 %all-gather.2.cloned.1.call-start = ((), (), s32[]{:S(2)}) async-start(), calls=%async_computation.3 | async-start | bytes 4325376 | tf_op jit(solution)/shard_map/while/body/eval_jaxpr/all_gather | solution.py:53
  1608.2 6.0 collective-permute-start
  1859.1 21.6 %reduce-scatter.2.cloned.1.call-start = ((), (), s32[]{:S(2)}) async-start(), calls=%async_computation.2 | async-start | bytes 655360 | tf_op jit(solution)/shard_map/reduce_scatter | solution.py:111
Sparse Core Ops, SparseCore 0:
  178.3 45.9 all-gather.1
  428.0 45.7 all-gather.1
  677.4 45.7 all-gather.1
  927.3 45.2 all-gather.1
  1178.9 44.1 all-gather.1
  1426.7 48.3 all-gather.1
  1678.8 48.1 all-gather.1
Sparse Core Ops, SparseCore 1:
  1862.5 18.2 reduce-scatter.1
where the time goes:
time: 1960 us; the launch traced here: 1950 us
  blocking collectives  1400 us (71%)
  waiting for transfers between devices  343 us (18%)
  other arithmetic  65.1 us (3%)
  matrix products  44.3 us (2%)
  local copies, waits for them, and re-layouts  41.1 us (2%)
  starting transfers between devices  32.5 us (2%)
    psum x7, blocking collectives, layer_of_section(): lax.psum(compressed_projection.astype(jnp.bfloat16), 'mp')  885 us
    psum x7, blocking collectives, layer_of_section(): squares = lax.psum(jnp.sum(hidden_f * hidden_f, axis=1), 'mp')  439 us
    all_gather x7, waiting for transfers between devices, layer_of_section(): gathered = lax.all_gather(rescaled_activation, 'mp', axis=1, tiled=True)  303 us
    psum x1, blocking collectives, shards(): raw = lax.psum(partial_score, 'mp')  64.6 us
    unnamed x2, other arithmetic  45.2 us
  transfers between devices with their start and end apart: 16, of which 16 were waited for; matrix products, arithmetic and copies ran while one was open for 1% of the time, Pallas kernels for 0%

commit v1 on v0

--- a/solution.py
+++ b/solution.py
@@ -1,9 +1,19 @@
+import functools
 import jax
 import jax.numpy as jnp
 from jax import lax
 from jax.sharding import PartitionSpec as P
 
 BLOCK = 128
+
+
+def _supply_all_core(v0, d_out):
+    return jnp.concatenate(
+        jax.lax.all_to_all(jnp.stack(jax.lax.axis_size("mp") * [v0], 0), "mp", 0, 0), d_out
+    )
+
+
+hubs_process = functools.partial(_supply_all_core, d_out=1)
 
 
 def shifted(value, axis, steps):
@@ -50,7 +60,7 @@
         rescaled_activation = (
             hidden_f * lax.rsqrt(squares / width + 1e-05)[:, None] * gain[None, :]
         ).astype(jnp.bfloat16)
-        gathered = lax.all_gather(rescaled_activation, "mp", axis=1, tiled=True)
+        gathered = hubs_process(rescaled_activation)
         base = jnp.dot(gathered, weight, preferred_element_type=jnp.float32)
         local_ids = adapter_numbers - owner_index * owned_blocks
         mine = (local_ids >= 0) & (local_ids < owned_blocks)

time: 1960 us -> 2150 us (1.097)
  local copies, waits for them, and re-layouts: 41.1 us -> 114 us
  waiting for transfers between devices: 343 us -> 405 us
  starting transfers between devices: 32.5 us -> 89.1 us
    all_to_all x0 -> x7, waiting for transfers between devices: none -> 356 us  [_supply_all_core(): jax.lax.all_to_all(jnp.stack(jax.lax.axis_size('mp') * [v0], 0), 'mp', 0, 0)]
    all_gather x7 -> x0, waiting for transfers between devices: 303 us -> none  [layer_of_section(): gathered = lax.all_gather(rescaled_activation, 'mp', axis=1, tiled=True)]
    all_to_all x0 -> x7, local copies, waits for them, and re-layouts: none -> 45 us  [_supply_all_core(): jax.lax.all_to_all(jnp.stack(jax.lax.axis_size('mp') * [v0], 0), 'mp', 0, 0)]
    all_to_all x0 -> x7, starting transfers between devices: none -> 33.9 us  [_supply_all_core(): jax.lax.all_to_all(jnp.stack(jax.lax.axis_size('mp') * [v0], 0), 'mp', 0, 0)]
    another operation x0 -> x8, local copies, waits for them, and re-layouts: none -> 24.7 us  [the longest x7 16.8 us: _supply_all_core(): jnp.stack(jax.lax.axis_size('mp') * [v0], 0)]
    ppermute x7, starting transfers between devices: 25.1 us -> 47.7 us  [shifted(): lax.ppermute(value, axis, [(source, source + steps) for source in range(i...]
  transfers between devices with their start and end apart: 16 -> 16, of which waited for: 16 -> 15; matrix products, arithmetic and copies ran while one was open for 1% -> 1% of each run, Pallas kernels for 0% -> 0%
where the time goes in v1:
time: 2150 us; the launch traced here: 2140 us
  blocking collectives  1410 us (66%)
  waiting for transfers between devices  405 us (19%)
  local copies, waits for them, and re-layouts  114 us (5%)
  starting transfers between devices  89.1 us (4%)
  other arithmetic  60.5 us (3%)
  matrix products  43.1 us (2%)
    psum x7, blocking collectives, layer_of_section(): lax.psum(compressed_projection.astype(jnp.bfloat16), 'mp')  888 us
    psum x7, blocking collectives, layer_of_section(): squares = lax.psum(jnp.sum(hidden_f * hidden_f, axis=1), 'mp')  439 us
    all_to_all x7, waiting for transfers between devices, _supply_all_core(): jax.lax.all_to_all(jnp.stack(jax.lax.axis_size('mp') * [v0], 0), 'mp', 0, 0)  356 us
    psum x1, blocking collectives, shards(): raw = lax.psum(partial_score, 'mp')  64.7 us
    ppermute x7, starting transfers between devices, shifted(): lax.ppermute(value, axis, [(source, source + steps) for source in range(i...  47.7 us
    unnamed x2, other arithmetic  45.2 us
    all_to_all x7, local copies, waits for them, and re-layouts, _supply_all_core(): jax.lax.all_to_all(jnp.stack(jax.lax.axis_size('mp') * [v0], 0), 'mp', 0, 0)  45 us
  transfers between devices with their start and end apart: 16, of which 15 were waited for; matrix products, arithmetic and copies ran while one was open for 1% of the time, Pallas kernels for 0%

profile of v1, /device:TPU:0, one launch (start us, length us, event | category | flops | bytes accessed | tf_op | source)
XLA Modules:
  0.0 2141.4 jit_solution(8399811046746629189)
XLA Ops:
  16.9 45.2 %reduce.1 = bf16[8192,64]{1,0:T(8,128)(2,1)S(1)} reduce(bf16[8192,1,1,64]{3,2,1,0:T(2,128)(2,1)} %bitcast.102, bf16[]{:T(256)} %broadcast.110), dimensions={1,2}, to_apply=%bitcast.56.reduce_sub_computation | reduce | bytes 2097154
  105.3 1932.2 %while.17 = (s32[]{:T(128)}, bf16[256,256]{1,0:T(8,128)(2,1)}, bf16[4,256,256]{2,1,0:T(8,128)(2,1)}, pred[]{:T(512)}, bf16[4,256,256]{2,1,0:T(8,128)(2,1)}, /*in...) while((s32[]{:T(128)}, bf16[256,256]{1,0:T(8,128)(2,1)}, ...), condition=%wide.region_8.9_spmd.clone, body=%wide.region_0.8_spmd.clone.sunk | while | flops 1353712128 | bytes 81862136 | solution.py:120
  113.2 63.4 %psum.36 = f32[256]{0:T(256)S(1)} all-reduce(f32[256]{0:T(256)S(1)} %get-tuple-element.513), channel_id=1, replica_groups=mesh['section'=4,'mp'=32] {'mp'}, use_global_device_ids=true, to_apply=%region_2.2 | all-reduce | flops 256 | bytes 2048 | tf_op jit(solution)/shard_map/while/body/eval_jaxpr/psum | solution.py:59
  187.0 50.9 %all-to-all-done = bf16[32,256,256]{2,1,0:T(8,128)(2,1)} async-done(((bf16[32,256,256]{2,1,0:T(8,128)(2,1)}), bf16[32,256,256]{2,1,0:T(8,128)(2,1)}, u32[]{:S(2)}, u32[]{:S(2)}) %all-to-all-start) | async-done | bytes 4194336 | tf_op jit(solution)/shard_map/while/body/eval_jaxpr/all_to_all | solution.py:12
  244.4 130.2 %psum.37 = bf16[2,128,64]{1,2,0:T(8,128)(2,1)S(1)} all-reduce(bf16[2,128,64]{1,2,0:T(8,128)(2,1)S(1)} %pad_maximum_fusion.2), channel_id=1, replica_groups=mesh['section'=4,'mp'=32] {'mp'}, use_global_device_ids=true, to_apply=%region_7.7 | all-reduce | flops 16384 | bytes 65536 | tf_op jit(solution)/shard_map/while/body/eval_jaxpr/psum | solution.py:87
  388.8 62.7 %psum.36 = f32[256]{0:T(256)S(1)} all-reduce(f32[256]{0:T(256)S(1)} %get-tuple-element.513), channel_id=1, replica_groups=mesh['section'=4,'mp'=32] {'mp'}, use_global_device_ids=true, to_apply=%region_2.2 | all-reduce | flops 256 | bytes 2048 | tf_op jit(solution)/shard_map/while/body/eval_jaxpr/psum | solution.py:59
  462.0 50.9 %all-to-all-done = bf16[32,256,256]{2,1,0:T(8,128)(2,1)} async-done(((bf16[32,256,256]{2,1,0:T(8,128)(2,1)}), bf16[32,256,256]{2,1,0:T(8,128)(2,1)}, u32[]{:S(2)}, u32[]{:S(2)}) %all-to-all-start) | async-done | bytes 4194336 | tf_op jit(solution)/shard_map/while/body/eval_jaxpr/all_to_all | solution.py:12
  531.3 123.8 %psum.37 = bf16[2,128,64]{1,2,0:T(8,128)(2,1)S(1)} all-reduce(bf16[2,128,64]{1,2,0:T(8,128)(2,1)S(1)} %pad_maximum_fusion.2), channel_id=1, replica_groups=mesh['section'=4,'mp'=32] {'mp'}, use_global_device_ids=true, to_apply=%region_7.7 | all-reduce | flops 16384 | bytes 65536 | tf_op jit(solution)/shard_map/while/body/eval_jaxpr/psum | solution.py:87
  666.6 62.7 %psum.36 = f32[256]{0:T(256)S(1)} all-reduce(f32[256]{0:T(256)S(1)} %get-tuple-element.513), channel_id=1, replica_groups=mesh['section'=4,'mp'=32] {'mp'}, use_global_device_ids=true, to_apply=%region_2.2 | all-reduce | flops 256 | bytes 2048 | tf_op jit(solution)/shard_map/while/body/eval_jaxpr/psum | solution.py:59
  739.7 50.9 %all-to-all-done = bf16[32,256,256]{2,1,0:T(8,128)(2,1)} async-done(((bf16[32,256,256]{2,1,0:T(8,128)(2,1)}), bf16[32,256,256]{2,1,0:T(8,128)(2,1)}, u32[]{:S(2)}, u32[]{:S(2)}) %all-to-all-start) | async-done | bytes 4194336 | tf_op jit(solution)/shard_map/while/body/eval_jaxpr/all_to_all | solution.py:12
  797.1 136.3 %psum.37 = bf16[2,128,64]{1,2,0:T(8,128)(2,1)S(1)} all-reduce(bf16[2,128,64]{1,2,0:T(8,128)(2,1)S(1)} %pad_maximum_fusion.2), channel_id=1, replica_groups=mesh['section'=4,'mp'=32] {'mp'}, use_global_device_ids=true, to_apply=%region_7.7 | all-reduce | flops 16384 | bytes 65536 | tf_op jit(solution)/shard_map/while/body/eval_jaxpr/psum | solution.py:87
  947.4 62.7 %psum.36 = f32[256]{0:T(256)S(1)} all-reduce(f32[256]{0:T(256)S(1)} %get-tuple-element.513), channel_id=1, replica_groups=mesh['section'=4,'mp'=32] {'mp'}, use_global_device_ids=true, to_apply=%region_2.2 | all-reduce | flops 256 | bytes 2048 | tf_op jit(solution)/shard_map/while/body/eval_jaxpr/psum | solution.py:59
  1020.5 50.9 %all-to-all-done = bf16[32,256,256]{2,1,0:T(8,128)(2,1)} async-done(((bf16[32,256,256]{2,1,0:T(8,128)(2,1)}), bf16[32,256,256]{2,1,0:T(8,128)(2,1)}, u32[]{:S(2)}, u32[]{:S(2)}) %all-to-all-start) | async-done | bytes 4194336 | tf_op jit(solution)/shard_map/while/body/eval_jaxpr/all_to_all | solution.py:12
  1077.9 124.3 %psum.37 = bf16[2,128,64]{1,2,0:T(8,128)(2,1)S(1)} all-reduce(bf16[2,128,64]{1,2,0:T(8,128)(2,1)S(1)} %pad_maximum_fusion.2), channel_id=1, replica_groups=mesh['section'=4,'mp'=32] {'mp'}, use_global_device_ids=true, to_apply=%region_7.7 | all-reduce | flops 16384 | bytes 65536 | tf_op jit(solution)/shard_map/while/body/eval_jaxpr/psum | solution.py:87
  1228.7 62.7 %psum.36 = f32[256]{0:T(256)S(1)} all-reduce(f32[256]{0:T(256)S(1)} %get-tuple-element.513), channel_id=1, replica_groups=mesh['section'=4,'mp'=32] {'mp'}, use_global_device_ids=true, to_apply=%region_2.2 | all-reduce | flops 256 | bytes 2048 | tf_op jit(solution)/shard_map/while/body/eval_jaxpr/psum | solution.py:59
  1301.9 50.9 %all-to-all-done = bf16[32,256,256]{2,1,0:T(8,128)(2,1)} async-done(((bf16[32,256,256]{2,1,0:T(8,128)(2,1)}), bf16[32,256,256]{2,1,0:T(8,128)(2,1)}, u32[]{:S(2)}, u32[]{:S(2)}) %all-to-all-start) | async-done | bytes 4194336 | tf_op jit(solution)/shard_map/while/body/eval_jaxpr/all_to_all | solution.py:12
  1359.2 124.3 %psum.37 = bf16[2,128,64]{1,2,0:T(8,128)(2,1)S(1)} all-reduce(bf16[2,128,64]{1,2,0:T(8,128)(2,1)S(1)} %pad_maximum_fusion.2), channel_id=1, replica_groups=mesh['section'=4,'mp'=32] {'mp'}, use_global_device_ids=true, to_apply=%region_7.7 | all-reduce | flops 16384 | bytes 65536 | tf_op jit(solution)/shard_map/while/body/eval_jaxpr/psum | solution.py:87
  1498.1 62.7 %psum.36 = f32[256]{0:T(256)S(1)} all-reduce(f32[256]{0:T(256)S(1)} %get-tuple-element.513), channel_id=1, replica_groups=mesh['section'=4,'mp'=32] {'mp'}, use_global_device_ids=true, to_apply=%region_2.2 | all-reduce | flops 256 | bytes 2048 | tf_op jit(solution)/shard_map/while/body/eval_jaxpr/psum | solution.py:59
  1571.2 50.9 %all-to-all-done = bf16[32,256,256]{2,1,0:T(8,128)(2,1)} async-done(((bf16[32,256,256]{2,1,0:T(8,128)(2,1)}), bf16[32,256,256]{2,1,0:T(8,128)(2,1)}, u32[]{:S(2)}, u32[]{:S(2)}) %all-to-all-start) | async-done | bytes 4194336 | tf_op jit(solution)/shard_map/while/body/eval_jaxpr/all_to_all | solution.py:12
  1628.5 124.3 %psum.37 = bf16[2,128,64]{1,2,0:T(8,128)(2,1)S(1)} all-reduce(bf16[2,128,64]{1,2,0:T(8,128)(2,1)S(1)} %pad_maximum_fusion.2), channel_id=1, replica_groups=mesh['section'=4,'mp'=32] {'mp'}, use_global_device_ids=true, to_apply=%region_7.7 | all-reduce | flops 16384 | bytes 65536 | tf_op jit(solution)/shard_map/while/body/eval_jaxpr/psum | solution.py:87
  1777.0 62.7 %psum.36 = f32[256]{0:T(256)S(1)} all-reduce(f32[256]{0:T(256)S(1)} %get-tuple-element.513), channel_id=1, replica_groups=mesh['section'=4,'mp'=32] {'mp'}, use_global_device_ids=true, to_apply=%region_2.2 | all-reduce | flops 256 | bytes 2048 | tf_op jit(solution)/shard_map/while/body/eval_jaxpr/psum | solution.py:59
  1850.1 50.9 %all-to-all-done = bf16[32,256,256]{2,1,0:T(8,128)(2,1)} async-done(((bf16[32,256,256]{2,1,0:T(8,128)(2,1)}), bf16[32,256,256]{2,1,0:T(8,128)(2,1)}, u32[]{:S(2)}, u32[]{:S(2)}) %all-to-all-start) | async-done | bytes 4194336 | tf_op jit(solution)/shard_map/while/body/eval_jaxpr/all_to_all | solution.py:12
  1907.4 124.3 %psum.37 = bf16[2,128,64]{1,2,0:T(8,128)(2,1)S(1)} all-reduce(bf16[2,128,64]{1,2,0:T(8,128)(2,1)S(1)} %pad_maximum_fusion.2), channel_id=1, replica_groups=mesh['section'=4,'mp'=32] {'mp'}, use_global_device_ids=true, to_apply=%region_7.7 | all-reduce | flops 16384 | bytes 65536 | tf_op jit(solution)/shard_map/while/body/eval_jaxpr/psum | solution.py:87
  2069.3 64.7 %psum.31 = f32[1,256]{1,0:T(1,128)S(1)} all-reduce(f32[1,256]{1,0:T(1,128)S(1)} %bitcast.108), channel_id=1, replica_groups=mesh['section'=4,'mp'=32] {'mp'}, use_global_device_ids=true, to_apply=%region_11.12 | all-reduce | flops 256 | bytes 2048 | tf_op jit(solution)/shard_map/psum | solution.py:130
  (176 shorter events, 337.0 us)
Async XLA Ops:
  64.3 24.6 %all-to-all-start.1 = ((bf16[32,2,8192]{2,1,0:T(2,128)(2,1)}), bf16[32,2,8192]{2,1,0:T(2,128)(2,1)S(1)}, u32[]{:S(2)}, u32[]{:S(2)}) async-start(bf16[32,2,8192]{2,1,0:T(2,128)(2,1)} %reshape.110), calls=%async_computation.1 | async-start | bytes 2097152 | tf_op jit(solution)/shard_map/all_to_all | solution.py:49
  71.8 2.1 copy-start.1
  71.8 2.2 copy-start.2
  71.8 2.2 copy-start
  71.8 1996.4 %reduce-scatter.2.cloned.1.call-start = ((), (), s32[]{:S(2)}) async-start(), calls=%async_computation.3 | async-start | bytes 655360 | tf_op jit(solution)/shard_map/reduce_scatter | solution.py:121
  105.3 1932.2 %copy-start.3 = (bf16[256]{0:T(256)(128)(2,1)S(1)}, bf16[256]{0:T(256)(128)(2,1)}, u32[]{:S(2)}) copy-start(bf16[256]{0:T(256)(128)(2,1)} %param.19) | copy-start | bytes 1540
  105.3 2028.7 %copy-start.4 = (s32[1,2]{1,0:T(1,128)S(1)}, s32[1,2]{1,0:T(1,128)}, u32[]{:S(2)}) copy-start(s32[1,2]{1,0:T(1,128)} %param.21) | copy-start | bytes 28
  105.3 6.8 collective-permute-start
  179.1 58.8 %all-to-all-start = ((bf16[32,256,256]{2,1,0:T(8,128)(2,1)}), bf16[32,256,256]{2,1,0:T(8,128)(2,1)}, u32[]{:S(2)}, u32[]{:S(2)}) async-start(bf16[32,256,256]{2,1,0:T(8,128)(2,1)} %stack.75), calls=%async_computation | async-start | bytes 8388608 | tf_op jit(solution)/shard_map/while/body/eval_jaxpr/all_to_all | solution.py:12
  381.2 6.6 collective-permute-start
  454.0 58.8 %all-to-all-start = ((bf16[32,256,256]{2,1,0:T(8,128)(2,1)}), bf16[32,256,256]{2,1,0:T(8,128)(2,1)}, u32[]{:S(2)}, u32[]{:S(2)}) async-start(bf16[32,256,256]{2,1,0:T(8,128)(2,1)} %stack.75), calls=%async_computation | async-start | bytes 8388608 | tf_op jit(solution)/shard_map/while/body/eval_jaxpr/all_to_all | solution.py:12
  527.2 1.6 slice-start
  661.7 3.8 collective-permute-start
  731.8 58.8 %all-to-all-start = ((bf16[32,256,256]{2,1,0:T(8,128)(2,1)}), bf16[32,256,256]{2,1,0:T(8,128)(2,1)}, u32[]{:S(2)}, u32[]{:S(2)}) async-start(bf16[32,256,256]{2,1,0:T(8,128)(2,1)} %stack.75), calls=%async_computation | async-start | bytes 8388608 | tf_op jit(solution)/shard_map/while/body/eval_jaxpr/all_to_all | solution.py:12
  940.0 6.3 collective-permute-start
  1012.6 58.8 %all-to-all-start = ((bf16[32,256,256]{2,1,0:T(8,128)(2,1)}), bf16[32,256,256]{2,1,0:T(8,128)(2,1)}, u32[]{:S(2)}, u32[]{:S(2)}) async-start(bf16[32,256,256]{2,1,0:T(8,128)(2,1)} %stack.75), calls=%async_computation | async-start | bytes 8388608 | tf_op jit(solution)/shard_map/while/body/eval_jaxpr/all_to_all | solution.py:12
  1208.8 18.9 collective-permute-start
  1293.9 58.8 %all-to-all-start = ((bf16[32,256,256]{2,1,0:T(8,128)(2,1)}), bf16[32,256,256]{2,1,0:T(8,128)(2,1)}, u32[]{:S(2)}, u32[]{:S(2)}) async-start(bf16[32,256,256]{2,1,0:T(8,128)(2,1)} %stack.75), calls=%async_computation | async-start | bytes 8388608 | tf_op jit(solution)/shard_map/while/body/eval_jaxpr/all_to_all | solution.py:12
  1490.2 6.9 collective-permute-start
  1563.3 58.8 %all-to-all-start = ((bf16[32,256,256]{2,1,0:T(8,128)(2,1)}), bf16[32,256,256]{2,1,0:T(8,128)(2,1)}, u32[]{:S(2)}, u32[]{:S(2)}) async-start(bf16[32,256,256]{2,1,0:T(8,128)(2,1)} %stack.75), calls=%async_computation | async-start | bytes 8388608 | tf_op jit(solution)/shard_map/while/body/eval_jaxpr/all_to_all | solution.py:12
  1759.5 16.4 collective-permute-start
  1842.2 58.8 %all-to-all-start = ((bf16[32,256,256]{2,1,0:T(8,128)(2,1)}), bf16[32,256,256]{2,1,0:T(8,128)(2,1)}, u32[]{:S(2)}, u32[]{:S(2)}) async-start(bf16[32,256,256]{2,1,0:T(8,128)(2,1)} %stack.75), calls=%async_computation | async-start | bytes 8388608 | tf_op jit(solution)/shard_map/while/body/eval_jaxpr/all_to_all | solution.py:12
Sparse Core Ops, SparseCore 0:
  2037.6 30.5 reduce-scatter.1
